TPU v7x, 512 devices: a whole 4x4x16 slice. The times are simulated.
512 devices in a mesh: blk: 512 (over y, z, x, core).
Axes of the slice: x: 4, y: 4, z: 16, core: 2. Of those that a mesh axis runs over, the one named last changes fastest.
Arguments:
- geometry: float32 [8, 524288], P(None, 'blk'), may hold values from -1 to 89.333333, as said below
- currents: float32 [32, 524288], P(None, 'blk'), may hold values from -6 to 6
- net_ids: int32 [524288], P('blk'), may hold values from 0 to 3
- pair_on: int32 [512, 8], P('blk'), may hold values from 0 to 1, as said below
Outputs:
- voltage: float32 [32, 524288], P(None, 'blk')
Inputs may be any that keep to these rules, and one draw needn't show every extreme that they name: `geometry`: rows 0 to 1 lie in 0 to 512 / 6 + 4, row 2 in 0 to 0.2, rows 3 to 5 form a unit vector, row 6 lies in 0.2 to 2 and row 7 in 0.05 to 0.5. Symmetric: pair_on[b, 4 + d - 1] equals pair_on[(b + d) mod 512, d - 1] for d = 1 .. 4.
All inputs are finite; a program needn't handle non-finite values.
Results may differ from a plain program's by a relative error of at most 0.0003.
Values sent between devices are 32-bit elements; how exact they have to be, the bound alone decides.
No kernel may reach another device: no remote copies, remote signals or barrier semaphores. Data moves between devices by JAX's collectives and lax.ppermute only.
A program may use at most 64 MiB of HBM per device.

v0:
```python
import functools

import jax
import jax.numpy as jnp
from jax import lax
from jax.experimental import pallas as pl
from jax.experimental.pallas import tpu as pltpu
from jax.sharding import PartitionSpec as P

F32 = jnp.float32
BF16 = jnp.bfloat16
NETS = 4
GEO = 8
COLS = 32
BLOCK = GEO + COLS
LANES = 128
ROWS = 512
VMEM = pl.BlockSpec(memory_space=pltpu.VMEM)
SMEM = pl.BlockSpec(memory_space=pltpu.SMEM)


def swap(block, pair_of):
    return lax.ppermute(block, "blk", [(i, pair_of(i)) for i in range(lax.axis_size("blk"))])


def in_two(value):
    high = value.astype(BF16)
    return high, (value - high.astype(F32)).astype(BF16)


def in_three(value):
    high = value.astype(BF16)
    rest = value - high.astype(F32)
    middle = rest.astype(BF16)
    return high, middle, (rest - middle.astype(F32)).astype(BF16)


def by_net(geo, moments, same, different):
    net = geo[7:8]
    rows = [moments * jnp.where(net == F32(n), F32(same), F32(different)) for n in range(NETS)]
    pad = jnp.zeros((16 - 3 * NETS, geo.shape[1]), F32)
    return jnp.concatenate(rows + [pad], axis=0)


def own_factor(geo):
    high, middle, low = in_three(by_net(geo, geo[4:7], 0.1, 0.05))
    return jnp.concatenate([high, high, middle, middle, high, low], axis=0)


def other_factor(geo, flag):
    moments = geo[4:7] if flag is None else geo[4:7] * flag
    high, middle, low = in_three(by_net(geo, moments, 1.0, 0.0))
    return jnp.concatenate([high, middle, high, middle, low, high], axis=0)


def pack_kernel(geometry, currents, nets, out):
    geo = geometry[...]
    z, radius = geo[2:3], geo[7:8]
    rows = [geo[0:3], z * z + radius * radius, geo[3:6] * geo[6:7], nets[...].astype(F32)]
    out[0:GEO] = jnp.concatenate(rows, axis=0)
    out[GEO:BLOCK] = currents[...]


def place():
    at = lax.axis_index("blk")
    return at & 1, (at >> 1) & 1, (at >> 2) & 1


def flag_at(flags, offset):
    return flags[0, jnp.where(offset < 0, -offset - 1, offset + 3)].astype(F32)


def add_tile(voltage, ref, first, flag, cols, left, right, cur):
    seg = left.shape[0]
    geo = ref[first : first + GEO]
    right[...] = other_factor(geo, flag)
    cur[...] = jnp.concatenate(in_two(ref[first + GEO : first + BLOCK]), axis=0)
    row_x, row_y = geo[0:1], geo[1:2]
    row_z, row_a = geo[2:3] * F32(-2.0), geo[3:4]

    def chunk(k, carry):
        at = pl.ds(pl.multiple_of(k * ROWS, ROWS), ROWS)
        wide = lambda q: jnp.tile(cols[q, at, :], (1, seg // LANES))
        moment = jnp.dot(left[at, :], right[...], preferred_element_type=F32)
        dx = wide(0) - row_x
        dy = wide(1) - row_y
        span = (wide(2) * row_z + (wide(3) + row_a)) + (dx * dx + dy * dy)
        high, low = in_two(moment * lax.rsqrt(span))
        nt = (((1,), (1,)), ((), ()))
        both = lax.dot_general(cur[...], high, nt, preferred_element_type=F32)
        rest = lax.dot_general(cur[0:COLS, :], low, nt, preferred_element_type=F32)
        voltage[:, at] += both[0:COLS] + both[COLS : 2 * COLS] + rest
        return carry

    lax.fori_loop(0, seg // ROWS, chunk, 0, unroll=True)


def spread(turned, cols):
    for q in range(4):
        cols[q] = jnp.broadcast_to(turned[:, q : q + 1], cols.shape[1:])


def own_kernel(own, voltage, turned, left, cols, right, cur):
    geo = own[0:GEO]
    turned[...] = jnp.transpose(geo)
    left[...] = jnp.transpose(own_factor(geo))
    spread(turned[...], cols)
    voltage[...] = jnp.zeros_like(voltage)
    add_tile(voltage, own, 0, None, cols, left, right, cur)


def others_kernel(offsets, flags, turned, left, before, *refs):
    blocks, (voltage, cols, right, cur) = refs[:-4], refs[-4:]
    spread(turned[...], cols)
    voltage[...] = before[...]
    found = [(ref, first) for ref in blocks for first in range(0, ref.shape[0], BLOCK)]
    for (ref, first), offset in zip(found, offsets, strict=True):
        add_tile(voltage, ref, first, flag_at(flags, offset(*place())), cols, left, right, cur)


def scratch(seg):
    return [
        pltpu.VMEM((4, seg, LANES), F32),
        pltpu.VMEM((96, seg), BF16),
        pltpu.VMEM((2 * COLS, seg), BF16),
    ]


def params(n, seg):
    return dict(
        compiler_params=pltpu.CompilerParams(vmem_limit_bytes=40 << 20),
        cost_estimate=pl.CostEstimate(
            flops=n * 6 * seg * seg * 192, bytes_accessed=n * BLOCK * seg * 4, transcendentals=n * seg * seg
        ),
    )


def own_tile(own):
    seg = own.shape[1]
    return pl.pallas_call(
        own_kernel,
        out_shape=(
            jax.ShapeDtypeStruct((COLS, seg), F32),
            jax.ShapeDtypeStruct((seg, GEO), F32),
            jax.ShapeDtypeStruct((seg, 96), BF16),
        ),
        in_specs=[VMEM],
        out_specs=(VMEM, VMEM, VMEM),
        scratch_shapes=scratch(seg),
        **params(1, seg),
    )(own)


def other_tiles(flags, turned, left, voltage, blocks, offsets):
    seg = left.shape[0]
    return pl.pallas_call(
        functools.partial(others_kernel, offsets),
        out_shape=jax.ShapeDtypeStruct((COLS, seg), F32),
        in_specs=[SMEM] + [VMEM] * (3 + len(blocks)),
        out_specs=VMEM,
        scratch_shapes=scratch(seg),
        **params(len(offsets), seg),
    )(flags, turned, left, voltage, *blocks)


def sign(bit):
    return 1 - 2 * bit


def shards(geometry, currents, net_ids, pair_on):
    seg = geometry.shape[1]
    packed = pl.pallas_call(
        pack_kernel,
        out_shape=jax.ShapeDtypeStruct((BLOCK, seg), F32),
        in_specs=[VMEM] * 3,
        out_specs=VMEM,
    )(geometry, currents, net_ids[None, :])
    n = lax.axis_size("blk")
    core, chip, half = place()
    within = swap(packed, lambda i: i ^ 4)
    across = swap(packed, lambda i: (((i - 4) % n ^ 4) + 4) % n)
    voltage, turned, left = own_tile(packed)
    within, across, voltage = lax.optimization_barrier((within, across, voltage))
    fourth = jnp.where(chip != half, across, within)
    second = swap(jnp.concatenate([packed, fourth], axis=0), lambda i: i ^ 2)
    voltage = other_tiles(
        pair_on,
        turned,
        left,
        voltage,
        [within, across],
        [lambda core, chip, half: 4 * sign(half), lambda core, chip, half: -4 * sign(half)],
    )
    second, voltage = lax.optimization_barrier((second, voltage))
    fourth = jnp.where(core != half, across, within)
    first = swap(jnp.concatenate([packed, fourth, second], axis=0), lambda i: i ^ 1)
    voltage = other_tiles(
        pair_on,
        turned,
        left,
        voltage,
        [second],
        [lambda core, chip, half: 2 * sign(chip), lambda core, chip, half: -2 * sign(chip)],
    )
    return other_tiles(
        pair_on,
        turned,
        left,
        voltage,
        [first],
        [
            lambda core, chip, half: sign(core),
            lambda core, chip, half: -3 * sign(core),
            lambda core, chip, half: sign(core) + 2 * sign(chip),
            lambda core, chip, half: sign(core) - 2 * sign(chip),
        ],
    )


def solution(mesh):
    return jax.shard_map(
        shards,
        mesh=mesh,
        in_specs=(P(None, "blk"), P(None, "blk"), P("blk"), P("blk", None)),
        out_specs=P(None, "blk"),
        check_vma=False,
    )
```

profile of v0, /device:TPU:1, one launch (start us, length us, event | category | flops | bytes accessed | tf_op | source)
XLA Modules:
  0.0 58.9 jit_solution(1975796271642352471)
XLA Ops:
  0.0 1.6 %shard_map.46.own = f32[40,1024]{1,0:T(8,128)} custom-call(f32[8,1024]{1,0:T(8,128)} %geometry.1, f32[32,1024]{1,0:T(8,128)} %currents.1, s32[1,1024]{1,0:T(1,128)} %bitcast.1), custom_call_target="tpu_custom_call" | custom-call | tf_op jit(solution)/shard_map/pallas_call | solution.py:172
  1.6 16.9 %collective-permute-start.1 = (f32[40,1024]{1,0:T(8,128)}, f32[40,1024]{1,0:T(8,128)S(1)}, u32[]{:S(2)}, u32[]{:S(2)}) collective-permute-start(f32[40,1024]{1,0:T(8,128)} %shard_map.46.own), channel_id=1, source_target_pairs={{0,508},{1,509},{2,510},{3,511},{4,8},{5,9},{6,10},{7,11},{8,4},{9... | collective-permute-start | bytes 491528 | tf_op jit(solution)/shard_map/ppermute | solution.py:23
  18.4 1.9 %collective-permute-start = (f32[40,1024]{1,0:T(8,128)}, f32[40,1024]{1,0:T(8,128)S(1)}, u32[]{:S(2)}, u32[]{:S(2)}) collective-permute-start(f32[40,1024]{1,0:T(8,128)} %shard_map.46.own), channel_id=1, source_target_pairs={{0,4},{1,5},{2,6},{3,7},{4,0},{5,1},{6,2},{7,3},{8,12},{9,13},{10,... | collective-permute-start | bytes 491528 | tf_op jit(solution)/shard_map/ppermute | solution.py:23
  20.4 0.0 copy-start
  20.4 0.9 %copy-done = f32[40,1024]{1,0:T(8,128)S(1)} copy-done((f32[40,1024]{1,0:T(8,128)S(1)}, f32[40,1024]{1,0:T(8,128)}, u32[]{:S(2)}) %copy-start) | copy-done | bytes 163864
  21.3 3.2 %shard_map.47 = (f32[32,1024]{1,0:T(8,128)S(1)}, f32[1024,8]{1,0:T(8,128)S(1)}, bf16[1024,96]{1,0:T(8,128)(2,1)S(1)}) custom-call(f32[40,1024]{1,0:T(8,128)S(1)} %copy-done), custom_call_target="tpu_custom_call" | custom-call | flops 1207959552 | bytes 163840 | tf_op jit(solution)/shard_map/pallas_call | solution.py:140
  24.4 0.0 collective-permute-done.1.refs_1_
  24.4 2.3 %collective-permute-done.refs_0_ = f32[40,1024]{1,0:T(8,128)S(1)} collective-permute-done((f32[40,1024]{1,0:T(8,128)}, f32[40,1024]{1,0:T(8,128)S(1)}, u32[]{:S(2)}, u32[]{:S(2)}) %collective-permute-start) | collective-permute-done | bytes 163872 | tf_op jit(solution)/shard_map/ppermute | solution.py:23
  26.8 2.2 %collective-permute-start.2 = (f32[80,1024]{1,0:T(8,128)S(1)}, f32[80,1024]{1,0:T(8,128)S(1)}, u32[]{:S(2)}, u32[]{:S(2)}) collective-permute-start(f32[80,1024]{1,0:T(8,128)S(1)} %pad_maximum_fusion.1), channel_id=1, source_target_pairs={{0,2},{1,3},{2,0},{3,1},{4,6},{5,7},{6,4},{7,5},{8,10},{9,11},{10,... | collective-permute-start | bytes 983048 | tf_op jit(solution)/shard_map/ppermute | solution.py:23
  29.1 0.0 copy-start.2
  29.1 0.6 %copy-done.2 = s32[1,8]{1,0:T(1,128)S(1)} copy-done((s32[1,8]{1,0:T(1,128)S(1)}, s32[1,8]{1,0:T(1,128)}, u32[]{:S(2)}) %copy-start.2) | copy-done | bytes 56
  29.7 0.0 copy-start.1
  29.7 5.9 %shard_map.48.before = f32[32,1024]{1,0:T(8,128)S(1)} custom-call(s32[1,8]{1,0:T(1,128)S(1)} %copy-done.2, f32[1024,8]{1,0:T(8,128)S(1)} %get-tuple-element.13.turned, bf16[1024,96]{1,0:T(8,128)(2,1)S(1)} %get-tuple-element.14.left, f32[32,1024]{1,0:T(8,128)S(1)} %get-tuple-element.18.before, f32[40,1024]{1,0:T(8,128)S(1)} %collective-permute-done.refs_0_, ...), custom_call_target="tpu_custom_call" | custom-call | flops 2415919104 | bytes 327680 | tf_op jit(solution)/shard_map/pallas_call | solution.py:156
  35.6 0.4 collective-permute-done.2.refs_0_
  36.1 0.0 copy-done.1
  36.1 0.1 pad_maximum_fusion
  36.1 4.9 %collective-permute-start.3 = (f32[160,1024]{1,0:T(8,128)S(1)}, f32[160,1024]{1,0:T(8,128)S(1)}, u32[]{:S(2)}, u32[]{:S(2)}) collective-permute-start(f32[160,1024]{1,0:T(8,128)S(1)} %pad_maximum_fusion), channel_id=1, source_target_pairs={{0,1},{1,0},{2,3},{3,2},{4,5},{5,4},{6,7},{7,6},{8,9},{9,8},{10,11... | collective-permute-start | bytes 1966088 | tf_op jit(solution)/shard_map/ppermute | solution.py:23
  41.0 6.0 %shard_map.49.before = f32[32,1024]{1,0:T(8,128)S(1)} custom-call(s32[1,8]{1,0:T(1,128)S(1)} %copy-done.2, f32[1024,8]{1,0:T(8,128)S(1)} %get-tuple-element.13.turned, bf16[1024,96]{1,0:T(8,128)(2,1)S(1)} %get-tuple-element.14.left, f32[32,1024]{1,0:T(8,128)S(1)} %shard_map.48.before, f32[80,1024]{1,0:T(8,128)S(1)} %collective-permute-done.2.refs_0_), custom_call_target="tpu_custom_call" | custom-call | flops 2415919104 | bytes 327680 | tf_op jit(solution)/shard_map/pallas_call | solution.py:156
  47.0 0.0 collective-permute-done.3.refs_0_
  47.1 11.9 %shard_map.50 = f32[32,1024]{1,0:T(8,128)} custom-call(s32[1,8]{1,0:T(1,128)S(1)} %copy-done.2, f32[1024,8]{1,0:T(8,128)S(1)} %get-tuple-element.13.turned, bf16[1024,96]{1,0:T(8,128)(2,1)S(1)} %get-tuple-element.14.left, f32[32,1024]{1,0:T(8,128)S(1)} %shard_map.49.before, f32[160,1024]{1,0:T(8,128)S(1)} %collective-permute-done.3.refs_0_), custom_call_target="tpu_custom_call" | custom-call | flops 4831838208 | bytes 655360 | tf_op jit(solution)/shard_map/pallas_call | solution.py:156
  (2 shorter events, 0.0 us)
Async XLA Ops:
  1.6 22.9 %collective-permute-start.1 = (f32[40,1024]{1,0:T(8,128)}, f32[40,1024]{1,0:T(8,128)S(1)}, u32[]{:S(2)}, u32[]{:S(2)}) collective-permute-start(f32[40,1024]{1,0:T(8,128)} %shard_map.46.own), channel_id=1, source_target_pairs={{0,508},{1,509},{2,510},{3,511},{4,8},{5,9},{6,10},{7,11},{8,4},{9... | collective-permute-start | bytes 491528 | tf_op jit(solution)/shard_map/ppermute | solution.py:23
  18.4 8.4 %collective-permute-start = (f32[40,1024]{1,0:T(8,128)}, f32[40,1024]{1,0:T(8,128)S(1)}, u32[]{:S(2)}, u32[]{:S(2)}) collective-permute-start(f32[40,1024]{1,0:T(8,128)} %shard_map.46.own), channel_id=1, source_target_pairs={{0,4},{1,5},{2,6},{3,7},{4,0},{5,1},{6,2},{7,3},{8,12},{9,13},{10,... | collective-permute-start | bytes 491528 | tf_op jit(solution)/shard_map/ppermute | solution.py:23
  20.4 0.9 %copy-start = (f32[40,1024]{1,0:T(8,128)S(1)}, f32[40,1024]{1,0:T(8,128)}, u32[]{:S(2)}) copy-start(f32[40,1024]{1,0:T(8,128)} %shard_map.46.own) | copy-start | bytes 491524
  26.8 9.2 %collective-permute-start.2 = (f32[80,1024]{1,0:T(8,128)S(1)}, f32[80,1024]{1,0:T(8,128)S(1)}, u32[]{:S(2)}, u32[]{:S(2)}) collective-permute-start(f32[80,1024]{1,0:T(8,128)S(1)} %pad_maximum_fusion.1), channel_id=1, source_target_pairs={{0,2},{1,3},{2,0},{3,1},{4,6},{5,7},{6,4},{7,5},{8,10},{9,11},{10,... | collective-permute-start | bytes 983048 | tf_op jit(solution)/shard_map/ppermute | solution.py:23
  29.1 0.7 %copy-start.2 = (s32[1,8]{1,0:T(1,128)S(1)}, s32[1,8]{1,0:T(1,128)}, u32[]{:S(2)}) copy-start(s32[1,8]{1,0:T(1,128)} %flags.5) | copy-start | bytes 100
  29.7 6.3 %copy-start.1 = (f32[40,1024]{1,0:T(8,128)S(1)}, f32[40,1024]{1,0:T(8,128)}, u32[]{:S(2)}) copy-start(f32[40,1024]{1,0:T(8,128)} %shard_map.46.own) | copy-start | bytes 491524
  36.1 10.9 %collective-permute-start.3 = (f32[160,1024]{1,0:T(8,128)S(1)}, f32[160,1024]{1,0:T(8,128)S(1)}, u32[]{:S(2)}, u32[]{:S(2)}) collective-permute-start(f32[160,1024]{1,0:T(8,128)S(1)} %pad_maximum_fusion), channel_id=1, source_target_pairs={{0,1},{1,0},{2,3},{3,2},{4,5},{5,4},{6,7},{7,6},{8,9},{9,8},{10,11... | collective-permute-start | bytes 1966088 | tf_op jit(solution)/shard_map/ppermute | solution.py:23
where the time goes:
time: 59.2 us; the launch traced here: 58.9 us
  Pallas kernels  28.5 us (48%)
  starting transfers between devices  25.9 us (44%)
  waiting for transfers between devices  2.83 us (5%)
  local copies, waits for them, and re-layouts  1.56 us (3%)
    ppermute x4, starting transfers between devices, swap(): lax.ppermute(block, 'blk', [(i, pair_of(i)) for i in range(lax.axis_size(...  25.9 us
    pallas_call x3, Pallas kernels, other_tiles(): pl.pallas_call(functools.partial(others_kernel, offsets), out_shape=jax.S...  23.8 us
    pallas_call x1, Pallas kernels, own_tile(): pl.pallas_call(own_kernel, out_shape=(jax.ShapeDtypeStruct((COLS, seg), F...  3.16 us
    ppermute x4, waiting for transfers between devices, swap(): lax.ppermute(block, 'blk', [(i, pair_of(i)) for i in range(lax.axis_size(...  2.83 us
    pallas_call x1, Pallas kernels, shards(): pl.pallas_call(pack_kernel, out_shape=jax.ShapeDtypeStruct((BLOCK, seg),...  1.57 us
    unnamed x6, local copies, waits for them, and re-layouts  1.56 us
  transfers between devices with their start and end apart: 4, of which 2 were waited for; matrix products, arithmetic and copies ran while one was open for 0% of the time, Pallas kernels for 26%

commit v1 on v0

v1 whole, which is shorter than its diff:
```python
import functools

import jax
import jax.numpy as jnp
from jax import lax
from jax.experimental import pallas as pl
from jax.experimental.pallas import tpu as pltpu
from jax.sharding import PartitionSpec as P

F32 = jnp.float32
BF16 = jnp.bfloat16
NETS = 4
GEO = 8
COLS = 32
BLOCK = GEO + COLS
LANES = 128
ROWS = 256
VMEM = pl.BlockSpec(memory_space=pltpu.VMEM)


def swap(block, pair_of):
    return lax.ppermute(block, "blk", [(i, pair_of(i)) for i in range(lax.axis_size("blk"))])


def in_two(value):
    high = value.astype(BF16)
    return high, (value - high.astype(F32)).astype(BF16)


def in_three(value):
    high = value.astype(BF16)
    rest = value - high.astype(F32)
    middle = rest.astype(BF16)
    return high, middle, (rest - middle.astype(F32)).astype(BF16)


def by_net(geo, moments, same, different):
    net = geo[7:8]
    rows = [moments * jnp.where(net == F32(n), F32(same), F32(different)) for n in range(NETS)]
    pad = jnp.zeros((16 - 3 * NETS, geo.shape[1]), F32)
    return jnp.concatenate(rows + [pad], axis=0)


def own_factor(geo):
    high, middle, low = in_three(by_net(geo, geo[4:7], 0.1, 0.05))
    return jnp.concatenate([high, high, middle, middle, high, low], axis=0)


def other_factor(geo, flag):
    moments = geo[4:7] if flag is None else geo[4:7] * flag
    high, middle, low = in_three(by_net(geo, moments, 1.0, 0.0))
    return jnp.concatenate([high, middle, high, middle, low, high], axis=0)


def pack(geometry, currents, nets, out):
    geo = geometry[...]
    z, radius = geo[2:3], geo[7:8]
    rows = [geo[0:3], z * z + radius * radius, geo[3:6] * geo[6:7], nets[...].astype(F32)]
    out[0:GEO] = jnp.concatenate(rows, axis=0)
    out[GEO:BLOCK] = currents[...]


def pack_kernel(geometry, currents, nets, pairs, out, flags):
    pack(geometry, currents, nets, out)
    flags[...] = jnp.transpose(jnp.broadcast_to(pairs[...], (LANES, pairs.shape[1])).astype(F32))


def place():
    at = lax.axis_index("blk")
    return at & 1, (at >> 1) & 1, (at >> 2) & 1


def flag_at(flags, offset):
    return flags[pl.ds(jnp.where(offset < 0, -offset - 1, offset + 3), 1), 0:1]


def add_tiles(voltage, blocks, cols, left, right, cur, moment, high, low):
    seg = left.shape[0]
    chunks = seg // ROWS
    steps = len(blocks) * chunks
    nt = (((1,), (1,)), ((), ()))

    def moments(step):
        block, chunk = divmod(step, chunks)
        ref, first, flag = blocks[block]
        if chunk == 0:
            right[block % 2] = other_factor(ref[first : first + GEO], flag)
            cur[block % 2] = jnp.concatenate(in_two(ref[first + GEO : first + BLOCK]), axis=0)
        rows = left[chunk * ROWS : (chunk + 1) * ROWS, :]
        moment[step % 2] = jnp.dot(rows, right[block % 2], preferred_element_type=F32)

    def kernel(step):
        block, chunk = divmod(step, chunks)
        ref, first, _ = blocks[block]
        at = slice(chunk * ROWS, (chunk + 1) * ROWS)
        wide = lambda q: jnp.tile(cols[q, at, :], (1, seg // LANES))
        row = lambda q: ref[first + q : first + q + 1]
        dx = wide(0) - row(0)
        dy = wide(1) - row(1)
        span = (wide(2) * (row(2) * F32(-2.0)) + (wide(3) + row(3))) + (dx * dx + dy * dy)
        high[step % 2], low[step % 2] = in_two(moment[step % 2] * lax.rsqrt(span))

    def induce(step):
        block, chunk = divmod(step, chunks)
        at = slice(chunk * ROWS, (chunk + 1) * ROWS)
        both = lax.dot_general(cur[block % 2], high[step % 2], nt, preferred_element_type=F32)
        rest = lax.dot_general(cur[block % 2, 0:COLS], low[step % 2], nt, preferred_element_type=F32)
        voltage[:, at] += both[0:COLS] + both[COLS : 2 * COLS] + rest

    for step in range(steps + 2):
        if step >= 2:
            induce(step - 2)
        if step < steps:
            moments(step)
        if 1 <= step <= steps:
            kernel(step - 1)


def spread(turned, cols):
    for q in range(4):
        cols[q] = jnp.broadcast_to(turned[:, q : q + 1], cols.shape[1:])


def own_kernel(geometry, currents, nets, voltage, turned, left, own, cols, *buffers):
    pack(geometry, currents, nets, own)
    geo = own[0:GEO]
    turned[...] = jnp.transpose(geo)
    left[...] = jnp.transpose(own_factor(geo))
    spread(turned[...], cols)
    voltage[...] = jnp.zeros_like(voltage)
    add_tiles(voltage, [(own, 0, None)], cols, left, *buffers)


def others_kernel(offsets, n_refs, flags, turned, left, before, *refs):
    found = [(ref, first) for ref in refs[:n_refs] for first in range(0, ref.shape[0], BLOCK)]
    voltage, cols, *buffers = refs[n_refs:]
    spread(turned[...], cols)
    voltage[...] = before[...]
    blocks = [
        (ref, first, flag_at(flags, offset(*place()))) for (ref, first), offset in zip(found, offsets, strict=True)
    ]
    add_tiles(voltage, blocks, cols, left, *buffers)


def scratch(seg):
    return [
        pltpu.VMEM((4, seg, LANES), F32),
        pltpu.VMEM((2, 96, seg), BF16),
        pltpu.VMEM((2, 2 * COLS, seg), BF16),
        pltpu.VMEM((2, ROWS, seg), F32),
        pltpu.VMEM((2, ROWS, seg), BF16),
        pltpu.VMEM((2, ROWS, seg), BF16),
    ]


def params(n, seg):
    return dict(
        compiler_params=pltpu.CompilerParams(vmem_limit_bytes=40 << 20),
        cost_estimate=pl.CostEstimate(
            flops=n * 6 * seg * seg * 192, bytes_accessed=n * BLOCK * seg * 4, transcendentals=n * seg * seg
        ),
    )


def own_tile(geometry, currents, nets):
    seg = geometry.shape[1]
    return pl.pallas_call(
        own_kernel,
        out_shape=(
            jax.ShapeDtypeStruct((COLS, seg), F32),
            jax.ShapeDtypeStruct((seg, GEO), F32),
            jax.ShapeDtypeStruct((seg, 96), BF16),
            jax.ShapeDtypeStruct((BLOCK, seg), F32),
        ),
        in_specs=[VMEM] * 3,
        out_specs=(VMEM,) * 4,
        scratch_shapes=scratch(seg),
        **params(1, seg),
    )(geometry, currents, nets)


def other_tiles(flags, turned, left, voltage, blocks, offsets):
    seg = left.shape[0]
    return pl.pallas_call(
        functools.partial(others_kernel, offsets, len(blocks)),
        out_shape=jax.ShapeDtypeStruct((COLS, seg), F32),
        in_specs=[VMEM] * (4 + len(blocks)),
        out_specs=VMEM,
        scratch_shapes=scratch(seg),
        **params(len(offsets), seg),
    )(flags, turned, left, voltage, *blocks)


def sign(bit):
    return 1 - 2 * bit


def shards(geometry, currents, net_ids, pair_on):
    seg = geometry.shape[1]
    nets = net_ids[None, :]
    packed, flags = pl.pallas_call(
        pack_kernel,
        out_shape=(
            jax.ShapeDtypeStruct((BLOCK, seg), F32),
            jax.ShapeDtypeStruct((pair_on.shape[1], LANES), F32),
        ),
        in_specs=[VMEM] * 4,
        out_specs=(VMEM, VMEM),
    )(geometry, currents, nets, pair_on)
    n = lax.axis_size("blk")
    core, chip, half = place()
    within = swap(packed, lambda i: i ^ 4)
    across = swap(packed, lambda i: (((i - 4) % n ^ 4) + 4) % n)
    voltage, turned, left, own = own_tile(geometry, currents, nets)
    within, across, voltage = lax.optimization_barrier((within, across, voltage))
    fourth = jnp.where(chip != half, across, within)
    second = swap(jnp.concatenate([own, fourth], axis=0), lambda i: i ^ 2)
    voltage = other_tiles(
        flags,
        turned,
        left,
        voltage,
        [within, across],
        [lambda core, chip, half: 4 * sign(half), lambda core, chip, half: -4 * sign(half)],
    )
    second, voltage = lax.optimization_barrier((second, voltage))
    fourth = jnp.where(core != half, across, within)
    first = swap(jnp.concatenate([own, fourth, second], axis=0), lambda i: i ^ 1)
    voltage = other_tiles(
        flags,
        turned,
        left,
        voltage,
        [second],
        [lambda core, chip, half: 2 * sign(chip), lambda core, chip, half: -2 * sign(chip)],
    )
    return other_tiles(
        flags,
        turned,
        left,
        voltage,
        [first],
        [
            lambda core, chip, half: sign(core),
            lambda core, chip, half: -3 * sign(core),
            lambda core, chip, half: sign(core) + 2 * sign(chip),
            lambda core, chip, half: sign(core) - 2 * sign(chip),
        ],
    )


def solution(mesh):
    return jax.shard_map(
        shards,
        mesh=mesh,
        in_specs=(P(None, "blk"), P(None, "blk"), P("blk"), P("blk", None)),
        out_specs=P(None, "blk"),
        check_vma=False,
    )
```

time: 59.2 us -> 56.2 us (0.949)
  Pallas kernels: 28.5 us -> 24.4 us
  waiting for transfers between devices: 2.83 us -> 4.81 us
  local copies, waits for them, and re-layouts: 1.56 us -> 0.67 us
    pallas_call x4, Pallas kernels: 25.3 us -> 21.4 us  [the longest x3 19.7 us: other_tiles(): pl.pallas_call(functools.partial(others_kernel, offsets, len(blocks)), ou...]
    ppermute x4, waiting for transfers between devices: 2.83 us -> 4.81 us  [swap(): lax.ppermute(block, 'blk', [(i, pair_of(i)) for i in range(lax.axis_size(...]
    unnamed x6 -> x8, local copies, waits for them, and re-layouts: 1.56 us -> 0.67 us
  transfers between devices with their start and end apart: 4 -> 4, of which waited for: 2 -> 2; matrix products, arithmetic and copies ran while one was open for 0% -> 0% of each run, Pallas kernels for 26% -> 23%
where the time goes in v1:
time: 56.2 us; the launch traced here: 56 us
  starting transfers between devices  25.9 us (46%)
  Pallas kernels  24.4 us (43%)
  waiting for transfers between devices  4.81 us (9%)
  local copies, waits for them, and re-layouts  0.67 us (1%)
    ppermute x4, starting transfers between devices, swap(): lax.ppermute(block, 'blk', [(i, pair_of(i)) for i in range(lax.axis_size(...  25.9 us
    pallas_call x3, Pallas kernels, other_tiles(): pl.pallas_call(functools.partial(others_kernel, offsets, len(blocks)), ou...  19.7 us
    ppermute x4, waiting for transfers between devices, swap(): lax.ppermute(block, 'blk', [(i, pair_of(i)) for i in range(lax.axis_size(...  4.81 us
    pallas_call x1, Pallas kernels, own_tile(): pl.pallas_call(own_kernel, out_shape=(jax.ShapeDtypeStruct((COLS, seg), F...  2.99 us
    pallas_call x1, Pallas kernels, shards(): pl.pallas_call(pack_kernel, out_shape=(jax.ShapeDtypeStruct((BLOCK, seg),...  1.65 us
  transfers between devices with their start and end apart: 4, of which 2 were waited for; matrix products, arithmetic and copies ran while one was open for 0% of the time, Pallas kernels for 23%

profile of v1, /device:TPU:1, one launch (start us, length us, event | category | flops | bytes accessed | tf_op | source)
XLA Modules:
  0.0 56.0 jit_solution(9934315943127701006)
XLA Ops:
  0.0 0.0 copy-start
  0.0 0.0 copy-start.1
  0.0 1.6 %shard_map.46 = (f32[40,1024]{1,0:T(8,128)}, f32[8,128]{1,0:T(8,128)}) custom-call(f32[8,1024]{1,0:T(8,128)} %geometry.3, f32[32,1024]{1,0:T(8,128)} %currents.3, s32[1,1024]{1,0:T(1,128)} %bitcast.1, s32[1,8]{1,0:T(1,128)} %pairs.1), custom_call_target="tpu_custom_call" | custom-call | tf_op jit(solution)/shard_map/pallas_call | solution.py:201
  1.7 16.9 %collective-permute-start.1 = (f32[40,1024]{1,0:T(8,128)}, f32[40,1024]{1,0:T(8,128)S(1)}, u32[]{:S(2)}, u32[]{:S(2)}) collective-permute-start(f32[40,1024]{1,0:T(8,128)} %get-tuple-element.20), channel_id=1, source_target_pairs={{0,508},{1,509},{2,510},{3,511},{4,8},{5,9},{6,10},{7,11},{8,4},{9... | collective-permute-start | bytes 491528 | tf_op jit(solution)/shard_map/ppermute | solution.py:22
  18.5 1.9 %collective-permute-start = (f32[40,1024]{1,0:T(8,128)}, f32[40,1024]{1,0:T(8,128)S(1)}, u32[]{:S(2)}, u32[]{:S(2)}) collective-permute-start(f32[40,1024]{1,0:T(8,128)} %get-tuple-element.20), channel_id=1, source_target_pairs={{0,4},{1,5},{2,6},{3,7},{4,0},{5,1},{6,2},{7,3},{8,12},{9,13},{10,... | collective-permute-start | bytes 491528 | tf_op jit(solution)/shard_map/ppermute | solution.py:22
  20.4 0.0 copy-start.2
  20.5 0.0 copy-done
  20.5 0.0 copy-done.1
  20.5 0.7 %copy-done.2 = s32[1024]{0:T(1024)S(1)} copy-done((s32[1024]{0:T(1024)S(1)}, s32[1024]{0:T(1024)}, u32[]{:S(2)}) %copy-start.2) | copy-done | bytes 4120
  21.1 3.0 %shard_map.47 = (f32[32,1024]{1,0:T(8,128)S(1)}, f32[1024,8]{1,0:T(8,128)S(1)}, bf16[1024,96]{1,0:T(8,128)(2,1)S(1)}, f32[40,1024]{1,0:T(8,128)S(1)}) custom-call(f32[8,1024]{1,0:T(8,128)S(1)} %copy-done.1, f32[32,1024]{1,0:T(8,128)S(1)} %copy-done, s32[1,1024]{1,0:T(1,128)S(1)} %bitcast.2), custom_call_target="tpu_custom_call" | custom-call | flops 1207959552 | bytes 163840 | tf_op jit(solution)/shard_map/pallas_call | solution.py:167
  24.1 0.0 collective-permute-done.1.refs_1_
  24.1 2.7 %collective-permute-done.refs_0_ = f32[40,1024]{1,0:T(8,128)S(1)} collective-permute-done((f32[40,1024]{1,0:T(8,128)}, f32[40,1024]{1,0:T(8,128)S(1)}, u32[]{:S(2)}, u32[]{:S(2)}) %collective-permute-start) | collective-permute-done | bytes 163872 | tf_op jit(solution)/shard_map/ppermute | solution.py:22
  26.9 0.0 copy-start.3
  26.9 2.2 %collective-permute-start.2 = (f32[80,1024]{1,0:T(8,128)S(1)}, f32[80,1024]{1,0:T(8,128)S(1)}, u32[]{:S(2)}, u32[]{:S(2)}) collective-permute-start(f32[80,1024]{1,0:T(8,128)S(1)} %pad_maximum_fusion.1), channel_id=1, source_target_pairs={{0,2},{1,3},{2,0},{3,1},{4,6},{5,7},{6,4},{7,5},{8,10},{9,11},{10,... | collective-permute-start | bytes 983048 | tf_op jit(solution)/shard_map/ppermute | solution.py:22
  29.2 0.0 copy-done.3
  29.2 4.9 %shard_map.48.before = f32[32,1024]{1,0:T(8,128)S(1)} custom-call(f32[8,128]{1,0:T(8,128)S(1)} %copy-done.3, f32[1024,8]{1,0:T(8,128)S(1)} %get-tuple-element.17.turned, bf16[1024,96]{1,0:T(8,128)(2,1)S(1)} %get-tuple-element.18.left, f32[32,1024]{1,0:T(8,128)S(1)} %get-tuple-element.24.before, f32[40,1024]{1,0:T(8,128)S(1)} %collective-permute-done.refs_0_, ...), custom_call_target="tpu_custom_call" | custom-call | flops 2415919104 | bytes 327680 | tf_op jit(solution)/shard_map/pallas_call | solution.py:184
  34.1 2.1 %collective-permute-done.2.refs_0_ = f32[80,1024]{1,0:T(8,128)S(1)} collective-permute-done((f32[80,1024]{1,0:T(8,128)S(1)}, f32[80,1024]{1,0:T(8,128)S(1)}, u32[]{:S(2)}, u32[]{:S(2)}) %collective-permute-start.2) | collective-permute-done | bytes 327712 | tf_op jit(solution)/shard_map/ppermute | solution.py:22
  36.2 0.1 pad_maximum_fusion
  36.2 4.9 %collective-permute-start.3 = (f32[160,1024]{1,0:T(8,128)S(1)}, f32[160,1024]{1,0:T(8,128)S(1)}, u32[]{:S(2)}, u32[]{:S(2)}) collective-permute-start(f32[160,1024]{1,0:T(8,128)S(1)} %pad_maximum_fusion), channel_id=1, source_target_pairs={{0,1},{1,0},{2,3},{3,2},{4,5},{5,4},{6,7},{7,6},{8,9},{9,8},{10,11... | collective-permute-start | bytes 1966088 | tf_op jit(solution)/shard_map/ppermute | solution.py:22
  41.1 4.9 %shard_map.49.before = f32[32,1024]{1,0:T(8,128)S(1)} custom-call(f32[8,128]{1,0:T(8,128)S(1)} %copy-done.3, f32[1024,8]{1,0:T(8,128)S(1)} %get-tuple-element.17.turned, bf16[1024,96]{1,0:T(8,128)(2,1)S(1)} %get-tuple-element.18.left, f32[32,1024]{1,0:T(8,128)S(1)} %shard_map.48.before, f32[80,1024]{1,0:T(8,128)S(1)} %collective-permute-done.2.refs_0_), custom_call_target="tpu_custom_call" | custom-call | flops 2415919104 | bytes 327680 | tf_op jit(solution)/shard_map/pallas_call | solution.py:184
  46.1 0.0 collective-permute-done.3.refs_0_
  46.1 9.9 %shard_map.50 = f32[32,1024]{1,0:T(8,128)} custom-call(f32[8,128]{1,0:T(8,128)S(1)} %copy-done.3, f32[1024,8]{1,0:T(8,128)S(1)} %get-tuple-element.17.turned, bf16[1024,96]{1,0:T(8,128)(2,1)S(1)} %get-tuple-element.18.left, f32[32,1024]{1,0:T(8,128)S(1)} %shard_map.49.before, f32[160,1024]{1,0:T(8,128)S(1)} %collective-permute-done.3.refs_0_), custom_call_target="tpu_custom_call" | custom-call | flops 4831838208 | bytes 655360 | tf_op jit(solution)/shard_map/pallas_call | solution.py:184
  (2 shorter events, 0.0 us)
Async XLA Ops:
  0.0 20.5 %copy-start = (f32[32,1024]{1,0:T(8,128)S(1)}, f32[32,1024]{1,0:T(8,128)}, u32[]{:S(2)}) copy-start(f32[32,1024]{1,0:T(8,128)} %currents.3) | copy-start | bytes 393220
  0.0 20.5 %copy-start.1 = (f32[8,1024]{1,0:T(8,128)S(1)}, f32[8,1024]{1,0:T(8,128)}, u32[]{:S(2)}) copy-start(f32[8,1024]{1,0:T(8,128)} %geometry.3) | copy-start | bytes 98308
  1.7 22.5 %collective-permute-start.1 = (f32[40,1024]{1,0:T(8,128)}, f32[40,1024]{1,0:T(8,128)S(1)}, u32[]{:S(2)}, u32[]{:S(2)}) collective-permute-start(f32[40,1024]{1,0:T(8,128)} %get-tuple-element.20), channel_id=1, source_target_pairs={{0,508},{1,509},{2,510},{3,511},{4,8},{5,9},{6,10},{7,11},{8,4},{9... | collective-permute-start | bytes 491528 | tf_op jit(solution)/shard_map/ppermute | solution.py:22
  18.5 8.4 %collective-permute-start = (f32[40,1024]{1,0:T(8,128)}, f32[40,1024]{1,0:T(8,128)S(1)}, u32[]{:S(2)}, u32[]{:S(2)}) collective-permute-start(f32[40,1024]{1,0:T(8,128)} %get-tuple-element.20), channel_id=1, source_target_pairs={{0,4},{1,5},{2,6},{3,7},{4,0},{5,1},{6,2},{7,3},{8,12},{9,13},{10,... | collective-permute-start | bytes 491528 | tf_op jit(solution)/shard_map/ppermute | solution.py:22
  20.4 0.7 %copy-start.2 = (s32[1024]{0:T(1024)S(1)}, s32[1024]{0:T(1024)}, u32[]{:S(2)}) copy-start(s32[1024]{0:T(1024)} %param.6) | copy-start | bytes 12292
  26.9 2.2 %copy-start.3 = (f32[8,128]{1,0:T(8,128)S(1)}, f32[8,128]{1,0:T(8,128)}, u32[]{:S(2)}) copy-start(f32[8,128]{1,0:T(8,128)} %get-tuple-element.16.flags) | copy-start | bytes 12292
  26.9 9.2 %collective-permute-start.2 = (f32[80,1024]{1,0:T(8,128)S(1)}, f32[80,1024]{1,0:T(8,128)S(1)}, u32[]{:S(2)}, u32[]{:S(2)}) collective-permute-start(f32[80,1024]{1,0:T(8,128)S(1)} %pad_maximum_fusion.1), channel_id=1, source_target_pairs={{0,2},{1,3},{2,0},{3,1},{4,6},{5,7},{6,4},{7,5},{8,10},{9,11},{10,... | collective-permute-start | bytes 983048 | tf_op jit(solution)/shard_map/ppermute | solution.py:22
  36.2 9.8 %collective-permute-start.3 = (f32[160,1024]{1,0:T(8,128)S(1)}, f32[160,1024]{1,0:T(8,128)S(1)}, u32[]{:S(2)}, u32[]{:S(2)}) collective-permute-start(f32[160,1024]{1,0:T(8,128)S(1)} %pad_maximum_fusion), channel_id=1, source_target_pairs={{0,1},{1,0},{2,3},{3,2},{4,5},{5,4},{6,7},{7,6},{8,9},{9,8},{10,11... | collective-permute-start | bytes 1966088 | tf_op jit(solution)/shard_map/ppermute | solution.py:22

commit v2 on v1

--- a/solution.py
+++ b/solution.py
@@ -121,8 +121,7 @@
         cols[q] = jnp.broadcast_to(turned[:, q : q + 1], cols.shape[1:])
 
 
-def own_kernel(geometry, currents, nets, voltage, turned, left, own, cols, *buffers):
-    pack(geometry, currents, nets, own)
+def own_kernel(own, voltage, turned, left, cols, *buffers):
     geo = own[0:GEO]
     turned[...] = jnp.transpose(geo)
     left[...] = jnp.transpose(own_factor(geo))
@@ -162,21 +161,20 @@
     )
 
 
-def own_tile(geometry, currents, nets):
-    seg = geometry.shape[1]
+def own_tile(own):
+    seg = own.shape[1]
     return pl.pallas_call(
         own_kernel,
         out_shape=(
             jax.ShapeDtypeStruct((COLS, seg), F32),
             jax.ShapeDtypeStruct((seg, GEO), F32),
             jax.ShapeDtypeStruct((seg, 96), BF16),
-            jax.ShapeDtypeStruct((BLOCK, seg), F32),
         ),
-        in_specs=[VMEM] * 3,
-        out_specs=(VMEM,) * 4,
+        in_specs=[VMEM],
+        out_specs=(VMEM,) * 3,
         scratch_shapes=scratch(seg),
         **params(1, seg),
-    )(geometry, currents, nets)
+    )(own)
 
 
 def other_tiles(flags, turned, left, voltage, blocks, offsets):
@@ -201,8 +199,8 @@
     packed, flags = pl.pallas_call(
         pack_kernel,
         out_shape=(
-            jax.ShapeDtypeStruct((BLOCK, seg), F32),
-            jax.ShapeDtypeStruct((pair_on.shape[1], LANES), F32),
+            pltpu.VMEM((BLOCK, seg), F32),
+            pltpu.VMEM((pair_on.shape[1], LANES), F32),
         ),
         in_specs=[VMEM] * 4,
         out_specs=(VMEM, VMEM),
@@ -211,21 +209,21 @@
     core, chip, half = place()
     within = swap(packed, lambda i: i ^ 4)
     across = swap(packed, lambda i: (((i - 4) % n ^ 4) + 4) % n)
-    voltage, turned, left, own = own_tile(geometry, currents, nets)
-    within, across, voltage = lax.optimization_barrier((within, across, voltage))
+    voltage, turned, left = own_tile(packed)
+    across, within, voltage = lax.optimization_barrier((across, within, voltage))
     fourth = jnp.where(chip != half, across, within)
-    second = swap(jnp.concatenate([own, fourth], axis=0), lambda i: i ^ 2)
+    second = swap(jnp.concatenate([packed, fourth], axis=0), lambda i: i ^ 2)
     voltage = other_tiles(
         flags,
         turned,
         left,
         voltage,
-        [within, across],
-        [lambda core, chip, half: 4 * sign(half), lambda core, chip, half: -4 * sign(half)],
+        [across, within],
+        [lambda core, chip, half: -4 * sign(half), lambda core, chip, half: 4 * sign(half)],
     )
     second, voltage = lax.optimization_barrier((second, voltage))
     fourth = jnp.where(core != half, across, within)
-    first = swap(jnp.concatenate([own, fourth, second], axis=0), lambda i: i ^ 1)
+    first = swap(jnp.concatenate([packed, fourth, second], axis=0), lambda i: i ^ 1)
     voltage = other_tiles(
         flags,
         turned,

time: 56.2 us -> 52.9 us (0.941)
  waiting for transfers between devices: 4.81 us -> 1.99 us
  starting transfers between devices: 25.9 us -> 26.8 us
  Pallas kernels: 24.4 us -> 23.7 us
  local copies, waits for them, and re-layouts: 0.67 us -> 0 us
    ppermute x4, waiting for transfers between devices: 4.81 us -> 1.99 us  [swap(): lax.ppermute(block, 'blk', [(i, pair_of(i)) for i in range(lax.axis_size(...]
    ppermute x4, starting transfers between devices: 25.9 us -> 26.8 us  [swap(): lax.ppermute(block, 'blk', [(i, pair_of(i)) for i in range(lax.axis_size(...]
    pallas_call x1, Pallas kernels: 1.65 us -> 0.97 us  [shards(): pl.pallas_call(pack_kernel, out_shape=(pltpu.VMEM((BLOCK, seg), F32), plt...]
    unnamed x8 -> x0, local copies, waits for them, and re-layouts: 0.67 us -> none
  transfers between devices with their start and end apart: 4 -> 4, of which waited for: 2 -> 2; matrix products, arithmetic and copies ran while one was open for 0% -> 0% of each run, Pallas kernels for 23% -> 24%
where the time goes in v2:
time: 52.9 us; the launch traced here: 52.6 us
  starting transfers between devices  26.8 us (51%)
  Pallas kernels  23.7 us (45%)
  waiting for transfers between devices  1.99 us (4%)
    ppermute x4, starting transfers between devices, swap(): lax.ppermute(block, 'blk', [(i, pair_of(i)) for i in range(lax.axis_size(...  26.8 us
    pallas_call x3, Pallas kernels, other_tiles(): pl.pallas_call(functools.partial(others_kernel, offsets, len(blocks)), ou...  19.7 us
    pallas_call x1, Pallas kernels, own_tile(): pl.pallas_call(own_kernel, out_shape=(jax.ShapeDtypeStruct((COLS, seg), F...  2.97 us
    ppermute x4, waiting for transfers between devices, swap(): lax.ppermute(block, 'blk', [(i, pair_of(i)) for i in range(lax.axis_size(...  1.99 us
  transfers between devices with their start and end apart: 4, of which 2 were waited for; matrix products, arithmetic and copies ran while one was open for 0% of the time, Pallas kernels for 24%

profile of v2, /device:TPU:1, one launch (start us, length us, event | category | flops | bytes accessed | tf_op | source)
XLA Modules:
  0.0 52.6 jit_solution(6114265384983600974)
XLA Ops:
  0.0 1.0 %shard_map.46 = (f32[40,1024]{1,0:T(8,128)S(1)}, f32[8,128]{1,0:T(8,128)S(1)}) custom-call(f32[8,1024]{1,0:T(8,128)} %geometry.1, f32[32,1024]{1,0:T(8,128)} %currents.1, s32[1,1024]{1,0:T(1,128)} %bitcast.1, s32[1,8]{1,0:T(1,128)} %pairs.1), custom_call_target="tpu_custom_call" | custom-call | tf_op jit(solution)/shard_map/pallas_call | solution.py:199
  1.0 5.5 %collective-permute-start.1 = (f32[40,1024]{1,0:T(8,128)S(1)}, f32[40,1024]{1,0:T(8,128)S(1)}, u32[]{:S(2)}, u32[]{:S(2)}) collective-permute-start(f32[40,1024]{1,0:T(8,128)S(1)} %get-tuple-element.16.own), channel_id=1, source_target_pairs={{0,4},{1,5},{2,6},{3,7},{4,0},{5,1},{6,2},{7,3},{8,12},{9,13},{10,... | collective-permute-start | bytes 491528 | tf_op jit(solution)/shard_map/ppermute | solution.py:22
  6.5 13.5 %collective-permute-start = (f32[40,1024]{1,0:T(8,128)S(1)}, f32[40,1024]{1,0:T(8,128)S(1)}, u32[]{:S(2)}, u32[]{:S(2)}) collective-permute-start(f32[40,1024]{1,0:T(8,128)S(1)} %get-tuple-element.16.own), channel_id=1, source_target_pairs={{0,508},{1,509},{2,510},{3,511},{4,8},{5,9},{6,10},{7,11},{8,4},{9... | collective-permute-start | bytes 491528 | tf_op jit(solution)/shard_map/ppermute | solution.py:22
  20.0 3.0 %shard_map.47 = (f32[32,1024]{1,0:T(8,128)S(1)}, f32[1024,8]{1,0:T(8,128)S(1)}, bf16[1024,96]{1,0:T(8,128)(2,1)S(1)}) custom-call(f32[40,1024]{1,0:T(8,128)S(1)} %get-tuple-element.16.own), custom_call_target="tpu_custom_call" | custom-call | flops 1207959552 | bytes 163840 | tf_op jit(solution)/shard_map/pallas_call | solution.py:166
  23.0 0.0 collective-permute-done.1.refs_1_
  23.0 0.6 %collective-permute-done.refs_0_ = f32[40,1024]{1,0:T(8,128)S(1)} collective-permute-done((f32[40,1024]{1,0:T(8,128)S(1)}, f32[40,1024]{1,0:T(8,128)S(1)}, u32[]{:S(2)}, u32[]{:S(2)}) %collective-permute-start) | collective-permute-done | bytes 163872 | tf_op jit(solution)/shard_map/ppermute | solution.py:22
  23.6 3.1 %collective-permute-start.2 = (f32[80,1024]{1,0:T(8,128)S(1)}, f32[80,1024]{1,0:T(8,128)S(1)}, u32[]{:S(2)}, u32[]{:S(2)}) collective-permute-start(f32[80,1024]{1,0:T(8,128)S(1)} %pad_maximum_fusion.1), channel_id=1, source_target_pairs={{0,2},{1,3},{2,0},{3,1},{4,6},{5,7},{6,4},{7,5},{8,10},{9,11},{10,... | collective-permute-start | bytes 983048 | tf_op jit(solution)/shard_map/ppermute | solution.py:22
  26.8 4.9 %shard_map.48.before = f32[32,1024]{1,0:T(8,128)S(1)} custom-call(f32[8,128]{1,0:T(8,128)S(1)} %get-tuple-element.15.flags, f32[1024,8]{1,0:T(8,128)S(1)} %get-tuple-element.17.turned, bf16[1024,96]{1,0:T(8,128)(2,1)S(1)} %get-tuple-element.18.left, f32[32,1024]{1,0:T(8,128)S(1)} %get-tuple-element.22.before, f32[40,1024]{1,0:T(8,128)S(1)} %collective-permute-done.refs_0_, ...), custom_call_target="tpu_custom_call" | custom-call | flops 2415919104 | bytes 327680 | tf_op jit(solution)/shard_map/pallas_call | solution.py:182
  31.7 1.4 %collective-permute-done.2.refs_0_ = f32[80,1024]{1,0:T(8,128)S(1)} collective-permute-done((f32[80,1024]{1,0:T(8,128)S(1)}, f32[80,1024]{1,0:T(8,128)S(1)}, u32[]{:S(2)}, u32[]{:S(2)}) %collective-permute-start.2) | collective-permute-done | bytes 327712 | tf_op jit(solution)/shard_map/ppermute | solution.py:22
  33.1 0.1 pad_maximum_fusion
  33.2 4.7 %collective-permute-start.3 = (f32[160,1024]{1,0:T(8,128)S(1)}, f32[160,1024]{1,0:T(8,128)S(1)}, u32[]{:S(2)}, u32[]{:S(2)}) collective-permute-start(f32[160,1024]{1,0:T(8,128)S(1)} %pad_maximum_fusion), channel_id=1, source_target_pairs={{0,1},{1,0},{2,3},{3,2},{4,5},{5,4},{6,7},{7,6},{8,9},{9,8},{10,11... | collective-permute-start | bytes 1966088 | tf_op jit(solution)/shard_map/ppermute | solution.py:22
  37.8 4.9 %shard_map.49.before = f32[32,1024]{1,0:T(8,128)S(1)} custom-call(f32[8,128]{1,0:T(8,128)S(1)} %get-tuple-element.15.flags, f32[1024,8]{1,0:T(8,128)S(1)} %get-tuple-element.17.turned, bf16[1024,96]{1,0:T(8,128)(2,1)S(1)} %get-tuple-element.18.left, f32[32,1024]{1,0:T(8,128)S(1)} %shard_map.48.before, f32[80,1024]{1,0:T(8,128)S(1)} %collective-permute-done.2.refs_0_), custom_call_target="tpu_custom_call" | custom-call | flops 2415919104 | bytes 327680 | tf_op jit(solution)/shard_map/pallas_call | solution.py:182
  42.8 0.0 collective-permute-done.3.refs_0_
  42.8 9.9 %shard_map.50 = f32[32,1024]{1,0:T(8,128)} custom-call(f32[8,128]{1,0:T(8,128)S(1)} %get-tuple-element.15.flags, f32[1024,8]{1,0:T(8,128)S(1)} %get-tuple-element.17.turned, bf16[1024,96]{1,0:T(8,128)(2,1)S(1)} %get-tuple-element.18.left, f32[32,1024]{1,0:T(8,128)S(1)} %shard_map.49.before, f32[160,1024]{1,0:T(8,128)S(1)} %collective-permute-done.3.refs_0_), custom_call_target="tpu_custom_call" | custom-call | flops 4831838208 | bytes 655360 | tf_op jit(solution)/shard_map/pallas_call | solution.py:182
  (2 shorter events, 0.1 us)
Async XLA Ops:
  1.0 22.0 %collective-permute-start.1 = (f32[40,1024]{1,0:T(8,128)S(1)}, f32[40,1024]{1,0:T(8,128)S(1)}, u32[]{:S(2)}, u32[]{:S(2)}) collective-permute-start(f32[40,1024]{1,0:T(8,128)S(1)} %get-tuple-element.16.own), channel_id=1, source_target_pairs={{0,4},{1,5},{2,6},{3,7},{4,0},{5,1},{6,2},{7,3},{8,12},{9,13},{10,... | collective-permute-start | bytes 491528 | tf_op jit(solution)/shard_map/ppermute | solution.py:22
  6.5 17.1 %collective-permute-start = (f32[40,1024]{1,0:T(8,128)S(1)}, f32[40,1024]{1,0:T(8,128)S(1)}, u32[]{:S(2)}, u32[]{:S(2)}) collective-permute-start(f32[40,1024]{1,0:T(8,128)S(1)} %get-tuple-element.16.own), channel_id=1, source_target_pairs={{0,508},{1,509},{2,510},{3,511},{4,8},{5,9},{6,10},{7,11},{8,4},{9... | collective-permute-start | bytes 491528 | tf_op jit(solution)/shard_map/ppermute | solution.py:22
  23.6 9.4 %collective-permute-start.2 = (f32[80,1024]{1,0:T(8,128)S(1)}, f32[80,1024]{1,0:T(8,128)S(1)}, u32[]{:S(2)}, u32[]{:S(2)}) collective-permute-start(f32[80,1024]{1,0:T(8,128)S(1)} %pad_maximum_fusion.1), channel_id=1, source_target_pairs={{0,2},{1,3},{2,0},{3,1},{4,6},{5,7},{6,4},{7,5},{8,10},{9,11},{10,... | collective-permute-start | bytes 983048 | tf_op jit(solution)/shard_map/ppermute | solution.py:22
  33.2 9.6 %collective-permute-start.3 = (f32[160,1024]{1,0:T(8,128)S(1)}, f32[160,1024]{1,0:T(8,128)S(1)}, u32[]{:S(2)}, u32[]{:S(2)}) collective-permute-start(f32[160,1024]{1,0:T(8,128)S(1)} %pad_maximum_fusion), channel_id=1, source_target_pairs={{0,1},{1,0},{2,3},{3,2},{4,5},{5,4},{6,7},{7,6},{8,9},{9,8},{10,11... | collective-permute-start | bytes 1966088 | tf_op jit(solution)/shard_map/ppermute | solution.py:22

commit v3 on v2

--- a/solution.py
+++ b/solution.py
@@ -76,35 +76,37 @@
 
 def add_tiles(voltage, blocks, cols, left, right, cur, moment, high, low):
     seg = left.shape[0]
-    chunks = seg // ROWS
-    steps = len(blocks) * chunks
     nt = (((1,), (1,)), ((), ()))
+    spans = [(block, first, ROWS) for block in range(len(blocks)) for first in range(0, seg, ROWS)]
+    block, first, size = spans.pop()
+    spans += [(block, first, size // 2), (block, first + size // 2, size // 2)]
+    steps = len(spans)
 
     def moments(step):
-        block, chunk = divmod(step, chunks)
+        block, start, size = spans[step]
         ref, first, flag = blocks[block]
-        if chunk == 0:
+        if start == 0:
             right[block % 2] = other_factor(ref[first : first + GEO], flag)
             cur[block % 2] = jnp.concatenate(in_two(ref[first + GEO : first + BLOCK]), axis=0)
-        rows = left[chunk * ROWS : (chunk + 1) * ROWS, :]
-        moment[step % 2] = jnp.dot(rows, right[block % 2], preferred_element_type=F32)
+        rows = left[start : start + size, :]
+        moment[step % 2, 0:size] = jnp.dot(rows, right[block % 2], preferred_element_type=F32)
 
     def kernel(step):
-        block, chunk = divmod(step, chunks)
+        block, start, size = spans[step]
         ref, first, _ = blocks[block]
-        at = slice(chunk * ROWS, (chunk + 1) * ROWS)
-        wide = lambda q: jnp.tile(cols[q, at, :], (1, seg // LANES))
+        wide = lambda q: jnp.tile(cols[q, start : start + size, :], (1, seg // LANES))
         row = lambda q: ref[first + q : first + q + 1]
         dx = wide(0) - row(0)
         dy = wide(1) - row(1)
         span = (wide(2) * (row(2) * F32(-2.0)) + (wide(3) + row(3))) + (dx * dx + dy * dy)
-        high[step % 2], low[step % 2] = in_two(moment[step % 2] * lax.rsqrt(span))
+        both = in_two(moment[step % 2, 0:size] * lax.rsqrt(span))
+        high[step % 2, 0:size], low[step % 2, 0:size] = both
 
     def induce(step):
-        block, chunk = divmod(step, chunks)
-        at = slice(chunk * ROWS, (chunk + 1) * ROWS)
-        both = lax.dot_general(cur[block % 2], high[step % 2], nt, preferred_element_type=F32)
-        rest = lax.dot_general(cur[block % 2, 0:COLS], low[step % 2], nt, preferred_element_type=F32)
+        block, start, size = spans[step]
+        at = slice(start, start + size)
+        both = lax.dot_general(cur[block % 2], high[step % 2, 0:size], nt, preferred_element_type=F32)
+        rest = lax.dot_general(cur[block % 2, 0:COLS], low[step % 2, 0:size], nt, preferred_element_type=F32)
         voltage[:, at] += both[0:COLS] + both[COLS : 2 * COLS] + rest
 
     for step in range(steps + 2):

time: 52.9 us -> 52.6 us (level)
  no operation moved by 1% of the time
where the time goes in v3:
time: 52.6 us; the launch traced here: 52.4 us
  starting transfers between devices  26.8 us (51%)
  Pallas kernels  23.4 us (44%)
  waiting for transfers between devices  2.04 us (4%)
    ppermute x4, starting transfers between devices, swap(): lax.ppermute(block, 'blk', [(i, pair_of(i)) for i in range(lax.axis_size(...  26.8 us
    pallas_call x3, Pallas kernels, other_tiles(): pl.pallas_call(functools.partial(others_kernel, offsets, len(blocks)), ou...  19.4 us
    pallas_call x1, Pallas kernels, own_tile(): pl.pallas_call(own_kernel, out_shape=(jax.ShapeDtypeStruct((COLS, seg), F...  3.04 us
    ppermute x4, waiting for transfers between devices, swap(): lax.ppermute(block, 'blk', [(i, pair_of(i)) for i in range(lax.axis_size(...  2.04 us
  transfers between devices with their start and end apart: 4, of which 2 were waited for; matrix products, arithmetic and copies ran while one was open for 0% of the time, Pallas kernels for 24%

profile of v3, /device:TPU:1, one launch (start us, length us, event | category | flops | bytes accessed | tf_op | source)
XLA Modules:
  0.0 52.4 jit_solution(6735255442977666890)
XLA Ops:
  0.0 1.0 %shard_map.46 = (f32[40,1024]{1,0:T(8,128)S(1)}, f32[8,128]{1,0:T(8,128)S(1)}) custom-call(f32[8,1024]{1,0:T(8,128)} %geometry.1, f32[32,1024]{1,0:T(8,128)} %currents.1, s32[1,1024]{1,0:T(1,128)} %bitcast.1, s32[1,8]{1,0:T(1,128)} %pairs.1), custom_call_target="tpu_custom_call" | custom-call | tf_op jit(solution)/shard_map/pallas_call | solution.py:201
  1.0 5.5 %collective-permute-start.1 = (f32[40,1024]{1,0:T(8,128)S(1)}, f32[40,1024]{1,0:T(8,128)S(1)}, u32[]{:S(2)}, u32[]{:S(2)}) collective-permute-start(f32[40,1024]{1,0:T(8,128)S(1)} %get-tuple-element.16.own), channel_id=1, source_target_pairs={{0,4},{1,5},{2,6},{3,7},{4,0},{5,1},{6,2},{7,3},{8,12},{9,13},{10,... | collective-permute-start | bytes 491528 | tf_op jit(solution)/shard_map/ppermute | solution.py:22
  6.5 13.5 %collective-permute-start = (f32[40,1024]{1,0:T(8,128)S(1)}, f32[40,1024]{1,0:T(8,128)S(1)}, u32[]{:S(2)}, u32[]{:S(2)}) collective-permute-start(f32[40,1024]{1,0:T(8,128)S(1)} %get-tuple-element.16.own), channel_id=1, source_target_pairs={{0,508},{1,509},{2,510},{3,511},{4,8},{5,9},{6,10},{7,11},{8,4},{9... | collective-permute-start | bytes 491528 | tf_op jit(solution)/shard_map/ppermute | solution.py:22
  20.0 3.0 %shard_map.47 = (f32[32,1024]{1,0:T(8,128)S(1)}, f32[1024,8]{1,0:T(8,128)S(1)}, bf16[1024,96]{1,0:T(8,128)(2,1)S(1)}) custom-call(f32[40,1024]{1,0:T(8,128)S(1)} %get-tuple-element.16.own), custom_call_target="tpu_custom_call" | custom-call | flops 1207959552 | bytes 163840 | tf_op jit(solution)/shard_map/pallas_call | solution.py:168
  23.0 0.0 collective-permute-done.1.refs_1_
  23.0 0.5 %collective-permute-done.refs_0_ = f32[40,1024]{1,0:T(8,128)S(1)} collective-permute-done((f32[40,1024]{1,0:T(8,128)S(1)}, f32[40,1024]{1,0:T(8,128)S(1)}, u32[]{:S(2)}, u32[]{:S(2)}) %collective-permute-start) | collective-permute-done | bytes 163872 | tf_op jit(solution)/shard_map/ppermute | solution.py:22
  23.6 3.1 %collective-permute-start.2 = (f32[80,1024]{1,0:T(8,128)S(1)}, f32[80,1024]{1,0:T(8,128)S(1)}, u32[]{:S(2)}, u32[]{:S(2)}) collective-permute-start(f32[80,1024]{1,0:T(8,128)S(1)} %pad_maximum_fusion.1), channel_id=1, source_target_pairs={{0,2},{1,3},{2,0},{3,1},{4,6},{5,7},{6,4},{7,5},{8,10},{9,11},{10,... | collective-permute-start | bytes 983048 | tf_op jit(solution)/shard_map/ppermute | solution.py:22
  26.8 4.8 %shard_map.48.before = f32[32,1024]{1,0:T(8,128)S(1)} custom-call(f32[8,128]{1,0:T(8,128)S(1)} %get-tuple-element.15.flags, f32[1024,8]{1,0:T(8,128)S(1)} %get-tuple-element.17.turned, bf16[1024,96]{1,0:T(8,128)(2,1)S(1)} %get-tuple-element.18.left, f32[32,1024]{1,0:T(8,128)S(1)} %get-tuple-element.22.before, f32[40,1024]{1,0:T(8,128)S(1)} %collective-permute-done.refs_0_, ...), custom_call_target="tpu_custom_call" | custom-call | flops 2415919104 | bytes 327680 | tf_op jit(solution)/shard_map/pallas_call | solution.py:184
  31.6 1.5 %collective-permute-done.2.refs_0_ = f32[80,1024]{1,0:T(8,128)S(1)} collective-permute-done((f32[80,1024]{1,0:T(8,128)S(1)}, f32[80,1024]{1,0:T(8,128)S(1)}, u32[]{:S(2)}, u32[]{:S(2)}) %collective-permute-start.2) | collective-permute-done | bytes 327712 | tf_op jit(solution)/shard_map/ppermute | solution.py:22
  33.1 0.1 pad_maximum_fusion
  33.2 4.7 %collective-permute-start.3 = (f32[160,1024]{1,0:T(8,128)S(1)}, f32[160,1024]{1,0:T(8,128)S(1)}, u32[]{:S(2)}, u32[]{:S(2)}) collective-permute-start(f32[160,1024]{1,0:T(8,128)S(1)} %pad_maximum_fusion), channel_id=1, source_target_pairs={{0,1},{1,0},{2,3},{3,2},{4,5},{5,4},{6,7},{7,6},{8,9},{9,8},{10,11... | collective-permute-start | bytes 1966088 | tf_op jit(solution)/shard_map/ppermute | solution.py:22
  37.8 4.8 %shard_map.49.before = f32[32,1024]{1,0:T(8,128)S(1)} custom-call(f32[8,128]{1,0:T(8,128)S(1)} %get-tuple-element.15.flags, f32[1024,8]{1,0:T(8,128)S(1)} %get-tuple-element.17.turned, bf16[1024,96]{1,0:T(8,128)(2,1)S(1)} %get-tuple-element.18.left, f32[32,1024]{1,0:T(8,128)S(1)} %shard_map.48.before, f32[80,1024]{1,0:T(8,128)S(1)} %collective-permute-done.2.refs_0_), custom_call_target="tpu_custom_call" | custom-call | flops 2415919104 | bytes 327680 | tf_op jit(solution)/shard_map/pallas_call | solution.py:184
  42.7 0.0 collective-permute-done.3.refs_0_
  42.7 9.8 %shard_map.50 = f32[32,1024]{1,0:T(8,128)} custom-call(f32[8,128]{1,0:T(8,128)S(1)} %get-tuple-element.15.flags, f32[1024,8]{1,0:T(8,128)S(1)} %get-tuple-element.17.turned, bf16[1024,96]{1,0:T(8,128)(2,1)S(1)} %get-tuple-element.18.left, f32[32,1024]{1,0:T(8,128)S(1)} %shard_map.49.before, f32[160,1024]{1,0:T(8,128)S(1)} %collective-permute-done.3.refs_0_), custom_call_target="tpu_custom_call" | custom-call | flops 4831838208 | bytes 655360 | tf_op jit(solution)/shard_map/pallas_call | solution.py:184
  (2 shorter events, 0.1 us)
Async XLA Ops:
  1.0 22.1 %collective-permute-start.1 = (f32[40,1024]{1,0:T(8,128)S(1)}, f32[40,1024]{1,0:T(8,128)S(1)}, u32[]{:S(2)}, u32[]{:S(2)}) collective-permute-start(f32[40,1024]{1,0:T(8,128)S(1)} %get-tuple-element.16.own), channel_id=1, source_target_pairs={{0,4},{1,5},{2,6},{3,7},{4,0},{5,1},{6,2},{7,3},{8,12},{9,13},{10,... | collective-permute-start | bytes 491528 | tf_op jit(solution)/shard_map/ppermute | solution.py:22
  6.5 17.1 %collective-permute-start = (f32[40,1024]{1,0:T(8,128)S(1)}, f32[40,1024]{1,0:T(8,128)S(1)}, u32[]{:S(2)}, u32[]{:S(2)}) collective-permute-start(f32[40,1024]{1,0:T(8,128)S(1)} %get-tuple-element.16.own), channel_id=1, source_target_pairs={{0,508},{1,509},{2,510},{3,511},{4,8},{5,9},{6,10},{7,11},{8,4},{9... | collective-permute-start | bytes 491528 | tf_op jit(solution)/shard_map/ppermute | solution.py:22
  23.6 9.4 %collective-permute-start.2 = (f32[80,1024]{1,0:T(8,128)S(1)}, f32[80,1024]{1,0:T(8,128)S(1)}, u32[]{:S(2)}, u32[]{:S(2)}) collective-permute-start(f32[80,1024]{1,0:T(8,128)S(1)} %pad_maximum_fusion.1), channel_id=1, source_target_pairs={{0,2},{1,3},{2,0},{3,1},{4,6},{5,7},{6,4},{7,5},{8,10},{9,11},{10,... | collective-permute-start | bytes 983048 | tf_op jit(solution)/shard_map/ppermute | solution.py:22
  33.2 9.5 %collective-permute-start.3 = (f32[160,1024]{1,0:T(8,128)S(1)}, f32[160,1024]{1,0:T(8,128)S(1)}, u32[]{:S(2)}, u32[]{:S(2)}) collective-permute-start(f32[160,1024]{1,0:T(8,128)S(1)} %pad_maximum_fusion), channel_id=1, source_target_pairs={{0,1},{1,0},{2,3},{3,2},{4,5},{5,4},{6,7},{7,6},{8,9},{9,8},{10,11... | collective-permute-start | bytes 1966088 | tf_op jit(solution)/shard_map/ppermute | solution.py:22

commit v4 on v3

--- a/solution.py
+++ b/solution.py
@@ -80,6 +80,8 @@
     spans = [(block, first, ROWS) for block in range(len(blocks)) for first in range(0, seg, ROWS)]
     block, first, size = spans.pop()
     spans += [(block, first, size // 2), (block, first + size // 2, size // 2)]
+    block, first, size = spans.pop(0)
+    spans = [(block, first, size // 2), (block, first + size // 2, size // 2)] + spans
     steps = len(spans)
 
     def moments(step):

time: 52.6 us -> 52.8 us (level)
  no operation moved by 1% of the time
where the time goes in v4:
time: 52.8 us; the launch traced here: 52.6 us
  starting transfers between devices  26.8 us (51%)
  Pallas kernels  23.7 us (45%)
  waiting for transfers between devices  1.95 us (4%)
    ppermute x4, starting transfers between devices, swap(): lax.ppermute(block, 'blk', [(i, pair_of(i)) for i in range(lax.axis_size(...  26.8 us
    pallas_call x3, Pallas kernels, other_tiles(): pl.pallas_call(functools.partial(others_kernel, offsets, len(blocks)), ou...  19.6 us
    pallas_call x1, Pallas kernels, own_tile(): pl.pallas_call(own_kernel, out_shape=(jax.ShapeDtypeStruct((COLS, seg), F...  3.06 us
    ppermute x4, waiting for transfers between devices, swap(): lax.ppermute(block, 'blk', [(i, pair_of(i)) for i in range(lax.axis_size(...  1.95 us
  transfers between devices with their start and end apart: 4, of which 2 were waited for; matrix products, arithmetic and copies ran while one was open for 0% of the time, Pallas kernels for 24%

profile of v4, /device:TPU:1, one launch (start us, length us, event | category | flops | bytes accessed | tf_op | source)
XLA Modules:
  0.0 52.6 jit_solution(51156864648441308)
XLA Ops:
  0.0 1.0 %shard_map.46 = (f32[40,1024]{1,0:T(8,128)S(1)}, f32[8,128]{1,0:T(8,128)S(1)}) custom-call(f32[8,1024]{1,0:T(8,128)} %geometry.1, f32[32,1024]{1,0:T(8,128)} %currents.1, s32[1,1024]{1,0:T(1,128)} %bitcast.1, s32[1,8]{1,0:T(1,128)} %pairs.1), custom_call_target="tpu_custom_call" | custom-call | tf_op jit(solution)/shard_map/pallas_call | solution.py:203
  1.0 5.5 %collective-permute-start.1 = (f32[40,1024]{1,0:T(8,128)S(1)}, f32[40,1024]{1,0:T(8,128)S(1)}, u32[]{:S(2)}, u32[]{:S(2)}) collective-permute-start(f32[40,1024]{1,0:T(8,128)S(1)} %get-tuple-element.16.own), channel_id=1, source_target_pairs={{0,4},{1,5},{2,6},{3,7},{4,0},{5,1},{6,2},{7,3},{8,12},{9,13},{10,... | collective-permute-start | bytes 491528 | tf_op jit(solution)/shard_map/ppermute | solution.py:22
  6.5 13.5 %collective-permute-start = (f32[40,1024]{1,0:T(8,128)S(1)}, f32[40,1024]{1,0:T(8,128)S(1)}, u32[]{:S(2)}, u32[]{:S(2)}) collective-permute-start(f32[40,1024]{1,0:T(8,128)S(1)} %get-tuple-element.16.own), channel_id=1, source_target_pairs={{0,508},{1,509},{2,510},{3,511},{4,8},{5,9},{6,10},{7,11},{8,4},{9... | collective-permute-start | bytes 491528 | tf_op jit(solution)/shard_map/ppermute | solution.py:22
  20.0 3.1 %shard_map.47 = (f32[32,1024]{1,0:T(8,128)S(1)}, f32[1024,8]{1,0:T(8,128)S(1)}, bf16[1024,96]{1,0:T(8,128)(2,1)S(1)}) custom-call(f32[40,1024]{1,0:T(8,128)S(1)} %get-tuple-element.16.own), custom_call_target="tpu_custom_call" | custom-call | flops 1207959552 | bytes 163840 | tf_op jit(solution)/shard_map/pallas_call | solution.py:170
  23.1 0.0 collective-permute-done.1.refs_1_
  23.1 0.5 collective-permute-done.refs_0_
  23.6 3.1 %collective-permute-start.2 = (f32[80,1024]{1,0:T(8,128)S(1)}, f32[80,1024]{1,0:T(8,128)S(1)}, u32[]{:S(2)}, u32[]{:S(2)}) collective-permute-start(f32[80,1024]{1,0:T(8,128)S(1)} %pad_maximum_fusion.1), channel_id=1, source_target_pairs={{0,2},{1,3},{2,0},{3,1},{4,6},{5,7},{6,4},{7,5},{8,10},{9,11},{10,... | collective-permute-start | bytes 983048 | tf_op jit(solution)/shard_map/ppermute | solution.py:22
  26.8 4.9 %shard_map.48.before = f32[32,1024]{1,0:T(8,128)S(1)} custom-call(f32[8,128]{1,0:T(8,128)S(1)} %get-tuple-element.15.flags, f32[1024,8]{1,0:T(8,128)S(1)} %get-tuple-element.17.turned, bf16[1024,96]{1,0:T(8,128)(2,1)S(1)} %get-tuple-element.18.left, f32[32,1024]{1,0:T(8,128)S(1)} %get-tuple-element.22.before, f32[40,1024]{1,0:T(8,128)S(1)} %collective-permute-done.refs_0_, ...), custom_call_target="tpu_custom_call" | custom-call | flops 2415919104 | bytes 327680 | tf_op jit(solution)/shard_map/pallas_call | solution.py:186
  31.7 1.4 %collective-permute-done.2.refs_0_ = f32[80,1024]{1,0:T(8,128)S(1)} collective-permute-done((f32[80,1024]{1,0:T(8,128)S(1)}, f32[80,1024]{1,0:T(8,128)S(1)}, u32[]{:S(2)}, u32[]{:S(2)}) %collective-permute-start.2) | collective-permute-done | bytes 327712 | tf_op jit(solution)/shard_map/ppermute | solution.py:22
  33.1 0.1 pad_maximum_fusion
  33.2 4.7 %collective-permute-start.3 = (f32[160,1024]{1,0:T(8,128)S(1)}, f32[160,1024]{1,0:T(8,128)S(1)}, u32[]{:S(2)}, u32[]{:S(2)}) collective-permute-start(f32[160,1024]{1,0:T(8,128)S(1)} %pad_maximum_fusion), channel_id=1, source_target_pairs={{0,1},{1,0},{2,3},{3,2},{4,5},{5,4},{6,7},{7,6},{8,9},{9,8},{10,11... | collective-permute-start | bytes 1966088 | tf_op jit(solution)/shard_map/ppermute | solution.py:22
  37.8 4.9 %shard_map.49.before = f32[32,1024]{1,0:T(8,128)S(1)} custom-call(f32[8,128]{1,0:T(8,128)S(1)} %get-tuple-element.15.flags, f32[1024,8]{1,0:T(8,128)S(1)} %get-tuple-element.17.turned, bf16[1024,96]{1,0:T(8,128)(2,1)S(1)} %get-tuple-element.18.left, f32[32,1024]{1,0:T(8,128)S(1)} %shard_map.48.before, f32[80,1024]{1,0:T(8,128)S(1)} %collective-permute-done.2.refs_0_), custom_call_target="tpu_custom_call" | custom-call | flops 2415919104 | bytes 327680 | tf_op jit(solution)/shard_map/pallas_call | solution.py:186
  42.7 0.0 collective-permute-done.3.refs_0_
  42.7 9.9 %shard_map.50 = f32[32,1024]{1,0:T(8,128)} custom-call(f32[8,128]{1,0:T(8,128)S(1)} %get-tuple-element.15.flags, f32[1024,8]{1,0:T(8,128)S(1)} %get-tuple-element.17.turned, bf16[1024,96]{1,0:T(8,128)(2,1)S(1)} %get-tuple-element.18.left, f32[32,1024]{1,0:T(8,128)S(1)} %shard_map.49.before, f32[160,1024]{1,0:T(8,128)S(1)} %collective-permute-done.3.refs_0_), custom_call_target="tpu_custom_call" | custom-call | flops 4831838208 | bytes 655360 | tf_op jit(solution)/shard_map/pallas_call | solution.py:186
  (2 shorter events, 0.1 us)
Async XLA Ops:
  1.0 22.1 %collective-permute-start.1 = (f32[40,1024]{1,0:T(8,128)S(1)}, f32[40,1024]{1,0:T(8,128)S(1)}, u32[]{:S(2)}, u32[]{:S(2)}) collective-permute-start(f32[40,1024]{1,0:T(8,128)S(1)} %get-tuple-element.16.own), channel_id=1, source_target_pairs={{0,4},{1,5},{2,6},{3,7},{4,0},{5,1},{6,2},{7,3},{8,12},{9,13},{10,... | collective-permute-start | bytes 491528 | tf_op jit(solution)/shard_map/ppermute | solution.py:22
  6.5 17.1 %collective-permute-start = (f32[40,1024]{1,0:T(8,128)S(1)}, f32[40,1024]{1,0:T(8,128)S(1)}, u32[]{:S(2)}, u32[]{:S(2)}) collective-permute-start(f32[40,1024]{1,0:T(8,128)S(1)} %get-tuple-element.16.own), channel_id=1, source_target_pairs={{0,508},{1,509},{2,510},{3,511},{4,8},{5,9},{6,10},{7,11},{8,4},{9... | collective-permute-start | bytes 491528 | tf_op jit(solution)/shard_map/ppermute | solution.py:22
  23.6 9.4 %collective-permute-start.2 = (f32[80,1024]{1,0:T(8,128)S(1)}, f32[80,1024]{1,0:T(8,128)S(1)}, u32[]{:S(2)}, u32[]{:S(2)}) collective-permute-start(f32[80,1024]{1,0:T(8,128)S(1)} %pad_maximum_fusion.1), channel_id=1, source_target_pairs={{0,2},{1,3},{2,0},{3,1},{4,6},{5,7},{6,4},{7,5},{8,10},{9,11},{10,... | collective-permute-start | bytes 983048 | tf_op jit(solution)/shard_map/ppermute | solution.py:22
  33.2 9.6 %collective-permute-start.3 = (f32[160,1024]{1,0:T(8,128)S(1)}, f32[160,1024]{1,0:T(8,128)S(1)}, u32[]{:S(2)}, u32[]{:S(2)}) collective-permute-start(f32[160,1024]{1,0:T(8,128)S(1)} %pad_maximum_fusion), channel_id=1, source_target_pairs={{0,1},{1,0},{2,3},{3,2},{4,5},{5,4},{6,7},{7,6},{8,9},{9,8},{10,11... | collective-permute-start | bytes 1966088 | tf_op jit(solution)/shard_map/ppermute | solution.py:22
